TPU v7x, 32 devices: a whole 2x2x4 slice. The times are simulated.
32 devices in a mesh: groups: 2 (over x), win: 4 (over y, core), rcv: 4 (over z).
Axes of the slice: x: 2, y: 2, z: 4, core: 2. Of those that a mesh axis runs over, the one named last changes fastest.
Arguments:
- traces: bfloat16 [32, 768, 4096], P('win', ('groups', 'rcv')), parts along dimension 1, may hold values from -6 to 6
- valid: int32 [64], P(('groups', 'win')), parts along dimension 0, may hold values 0 or 1
- src_station: int32 [64], P('groups'), parts along dimension 0, may hold values from 0 to 383, as said below
Outputs:
- stacks: float32 [32, 768, 2, 512], P(None, ('groups', 'rcv'), None, 'win'), parts along dimension 1
There are 2 independent parts, one for each index of `groups`. A program takes and returns all parts, laid end to end along the dimension named above; each array names one. Nothing has to cross between parts.
Inputs may be any that keep to these rules, and one draw needn't show every extreme that they name: `src_station`: distinct stations; station 0 and station 384 - 1 are always among them.
All inputs are finite; a program needn't handle non-finite values. No bound on the sum of `valid` on one device may be relied on, other than what follows from the above.
Results may differ from a plain program's by a relative error of at most 0.0049.
Values may be sent and summed in bfloat16 or wider, within the bound.
A program may use at most 128 MiB of HBM per device.

v0:
```python
import math
import jax
import jax.numpy as jnp
import ml_dtypes
import numpy as np
from jax import lax
from jax.sharding import PartitionSpec as P

F = 512


def band_table(count, bins, first):
    samples = np.arange(count, dtype=np.int64)
    freqs = first + np.arange(bins, dtype=np.int64)
    phase = samples[:, None] * freqs[None, :] % count
    angle = phase.astype(np.float64) * (2.0 * math.pi / count)
    return np.concatenate([np.cos(angle), -np.sin(angle)], axis=1).astype(ml_dtypes.bfloat16)


def body(traces, valid, src_station):
    w_dev, r_dev, samples = traces.shape
    bins = F
    n_win = lax.axis_size("win")
    f_dev = bins // n_win
    table = jnp.asarray(band_table(samples, bins, samples // 16))
    spectra = jnp.dot(
        traces.reshape(w_dev * r_dev, samples), table, preferred_element_type=jnp.float32
    )
    power = jnp.sum(spectra * spectra, axis=1, keepdims=True) / bins
    keep = jnp.repeat(valid.astype(jnp.float32), r_dev)[:, None]
    white = (spectra * (lax.rsqrt(power + 1e-06) * keep)).astype(jnp.bfloat16)
    white = white.reshape(w_dev * r_dev, 2, n_win, f_dev)
    pieces = jnp.transpose(white, (2, 1, 0, 3))
    got = lax.all_to_all(pieces, "win", 0, 0, tiled=True)
    got = got.reshape(n_win, 2, w_dev, r_dev, f_dev)
    offset = lax.axis_index("rcv") * r_dev
    station_ids = offset + jnp.arange(r_dev, dtype=jnp.int32)
    selector = (src_station[:, None] == station_ids[None, :]).astype(jnp.bfloat16)
    rows = jnp.einsum("sr,gcwrf->gcwsf", selector, got, preferred_element_type=jnp.float32)
    src = lax.psum(rows.astype(jnp.bfloat16), "rcv")
    scale = 1.0 / math.sqrt(w_dev * n_win)
    turned = jnp.stack([got[:, 1], -got[:, 0]], axis=1)
    real = jnp.einsum("gcwsf,gcwrf->srf", src, got, preferred_element_type=jnp.float32)
    imag = jnp.einsum("gcwsf,gcwrf->srf", src, turned, preferred_element_type=jnp.float32)
    return jnp.stack([real, imag], axis=2) * scale


def solution(mesh):
    return jax.shard_map(
        body,
        mesh=mesh,
        in_specs=(P("win", ("groups", "rcv"), None), P(("groups", "win")), P("groups")),
        out_specs=P(None, ("groups", "rcv"), None, "win"),
        check_vma=False,
    )
```

profile of v0, /device:TPU:0, one launch (start us, length us, event | category | flops | bytes accessed | tf_op | source)
XLA Modules:
  0.0 113.4 jit_solution(5430483913655910019)
XLA Ops:
  6.5 0.7 convert_element_type.13
  7.2 0.1 broadcast_in_dim.2
  7.3 0.1 broadcast_in_dim_reshape.3
  7.3 11.0 %multiply_reduce_fusion = (f32[768]{0:T(1024)S(1)}, f32[1024,768]{1,0:T(8,128)S(1)}) fusion(bf16[4096,1024]{1,0:T(8,128)(2,1)} %constant.17.clone, bf16[768,4096]{1,0:T(8,128)(2,1)} %bitcast.42), kind=kOutput, calls=%fused_computation.2 | convolution fusion | flops 6444022784 | bytes 17828864 | tf_op jit(solution)/shard_map/dot_general | solution.py:26
  18.4 0.3 multiply_convert_fusion
  18.7 1.3 %copy.31 = bf16[768,2,4,128]{0,3,1,2:T(8,128)(2,1)} copy(bf16[768,2,4,128]{0,3,2,1:T(8,128)(2,1)S(1)} %bitcast.41) | data formatting | bytes 3145728 | tf_op jit(solution)/shard_map/reshape | solution.py:32
  19.9 4.2 %all-to-all-start = ((bf16[4,2,768,128]{2,3,1,0:T(8,128)(2,1)}), bf16[4,2,768,128]{2,3,1,0:T(8,128)(2,1)S(1)}, u32[]{:S(2)}, u32[]{:S(2)}) async-start(bf16[4,2,768,128]{2,3,1,0:T(8,128)(2,1)} %bitcast.35), calls=%async_computation | async-start | bytes 3145728 | tf_op jit(solution)/shard_map/all_to_all | solution.py:34
  24.2 0.0 copy-start.1
  24.2 0.0 all-reduce.2.cloned.1.call-start
  24.2 20.1 %all-to-all-done = bf16[4,2,768,128]{2,3,1,0:T(8,128)(2,1)S(1)} async-done(((bf16[4,2,768,128]{2,3,1,0:T(8,128)(2,1)}), bf16[4,2,768,128]{2,3,1,0:T(8,128)(2,1)S(1)}, u32[]{:S(2)}, u32[]{:S(2)}) %all-to-all-start) | async-done | bytes 1572896 | tf_op jit(solution)/shard_map/all_to_all | solution.py:34
  44.2 0.9 copy.19
  45.1 0.0 copy-done.1
  45.2 1.2 %fusion = bf16[4,2,8,32,128]{4,3,2,1,0:T(8,128)(2,1)} fusion(bf16[4,2,8,96,128]{4,3,2,1,0:T(8,128)(2,1)S(1)} %bitcast.36, s32[96]{0:T(128)S(1)} %iota_add_fusion, s32[32]{0:T(128)S(1)} %copy-done.1), kind=kOutput, calls=%fused_computation.8 | convolution fusion | flops 50596864 | bytes 2097664 | tf_op jit(solution)/shard_map/sr,gcwrf->gcwsf/dot_general | solution.py:39
  46.4 0.0 all-reduce.2.cloned.1.call-update
  46.4 3.0 %copy.20 = bf16[4,2,8,96,128]{3,2,0,1,4:T(8,128)(2,1)} copy(bf16[4,2,8,96,128]{4,3,2,1,0:T(8,128)(2,1)S(1)} %bitcast.37) | data formatting | bytes 3145728 | tf_op jit(solution)/shard_map/reshape | solution.py:35
  49.4 0.2 fusion.5
  49.5 0.1 pad_maximum_fusion
  49.7 2.9 %copy.23 = bf16[4,2,8,96,128]{3,2,0,1,4:T(8,128)(2,1)} copy(bf16[4,2,8,96,128]{4,3,2,1,0:T(8,128)(2,1)S(1)} %pad_maximum_fusion) | data formatting | bytes 3145728 | tf_op jit(solution)/shard_map/stack | solution.py:42
  52.6 33.3 %all-reduce.2.cloned.1.call-done = bf16[4,2,8,32,128]{4,3,2,1,0:T(8,128)(2,1)} async-done(((bf16[4,2,8,32,128]{4,3,2,1,0:T(8,128)(2,1)}), bf16[4,2,8,32,128]{4,3,2,1,0:T(8,128)(2,1)}) %all-reduce.2.cloned.1.call-update) | async-done | bytes 524304 | tf_op jit(solution)/shard_map/psum | solution.py:40
  85.8 3.9 %copy.21 = bf16[4,2,8,32,128]{3,2,0,1,4:T(8,128)(2,1)S(1)} copy(bf16[4,2,8,32,128]{4,3,2,1,0:T(8,128)(2,1)} %all-reduce.2.cloned.1.call-done) | data formatting | bytes 1048576 | tf_op jit(solution)/shard_map/psum | solution.py:40
  89.7 3.6 %convolution_bitcast_fusion = f32[128,96,32]{1,2,0:T(8,128)} fusion(bf16[4,2,8,96,128]{3,2,0,1,4:T(8,128)(2,1)} %copy.23, bf16[4,2,8,32,128]{3,2,0,1,4:T(8,128)(2,1)S(1)} %copy.21), kind=kOutput, calls=%fused_computation.3 | convolution fusion | flops 50331648 | bytes 3670016 | tf_op jit(solution)/shard_map/gcwsf,gcwrf->srf/dot_general | solution.py:44
  93.4 2.9 %copy.25 = f32[128,96,32]{0,1,2:T(8,128)} copy(f32[128,96,32]{1,2,0:T(8,128)} %convolution_bitcast_fusion) | data formatting | bytes 3145728 | tf_op jit(solution)/shard_map/gcwsf,gcwrf->srf/dot_general | solution.py:44
  96.3 3.6 %convolution_bitcast_fusion.1 = f32[128,96,32]{1,2,0:T(8,128)} fusion(bf16[4,2,8,96,128]{3,2,0,1,4:T(8,128)(2,1)} %copy.20, bf16[4,2,8,32,128]{3,2,0,1,4:T(8,128)(2,1)S(1)} %copy.21), kind=kOutput, calls=%fused_computation.4 | convolution fusion | flops 50331648 | bytes 3670016 | tf_op jit(solution)/shard_map/gcwsf,gcwrf->srf/dot_general | solution.py:43
  100.0 0.0 copy-start
  100.0 2.2 %copy.22 = f32[128,96,32]{0,1,2:T(8,128)S(1)} copy(f32[128,96,32]{1,2,0:T(8,128)} %convolution_bitcast_fusion.1) | data formatting | bytes 3145728 | tf_op jit(solution)/shard_map/gcwsf,gcwrf->srf/dot_general | solution.py:43
  102.1 0.0 copy-done
  102.1 0.3 maximum_multiply_fusion
  102.5 4.1 %copy.26 = f32[32,96,2,128]{3,2,1,0:T(2,128)} copy(f32[32,96,2,128]{3,1,2,0:T(8,128)S(1)} %maximum_multiply_fusion) | data formatting | bytes 6291456 | tf_op jit(solution)/shard_map/mul | solution.py:45
  (2 shorter events, 0.0 us)
Async XLA Ops:
  19.9 24.3 %all-to-all-start = ((bf16[4,2,768,128]{2,3,1,0:T(8,128)(2,1)}), bf16[4,2,768,128]{2,3,1,0:T(8,128)(2,1)S(1)}, u32[]{:S(2)}, u32[]{:S(2)}) async-start(bf16[4,2,768,128]{2,3,1,0:T(8,128)(2,1)} %bitcast.35), calls=%async_computation | async-start | bytes 3145728 | tf_op jit(solution)/shard_map/all_to_all | solution.py:34
  24.2 21.0 %copy-start.1 = (s32[32]{0:T(128)S(1)}, s32[32]{0:T(128)}, u32[]{:S(2)}) copy-start(s32[32]{0:T(128)} %param.6) | copy-start | bytes 388
  24.2 61.7 %all-reduce.2.cloned.1.call-start = ((), (), s32[]{:S(2)}) async-start(), calls=%async_computation.1 | async-start | bytes 1048576 | tf_op jit(solution)/shard_map/psum | solution.py:40
  100.0 2.2 %copy-start = (f32[128,96,32]{0,1,2:T(8,128)S(1)}, f32[128,96,32]{0,1,2:T(8,128)}, u32[]{:S(2)}) copy-start(f32[128,96,32]{0,1,2:T(8,128)} %copy.25) | copy-start | bytes 4718596
Sparse Core Ops, SparseCore 0:
  46.5 39.2 all-reduce.1
where the time goes:
time: 114 us; the launch traced here: 113 us
  waiting for transfers between devices  53.4 us (47%)
  local copies, waits for them, and re-layouts  21.2 us (19%)
  matrix products  19.5 us (17%)
  between operations  13.5 us (12%)
  starting transfers between devices  4.24 us (4%)
  other arithmetic  1.54 us (1%)
    psum x1, waiting for transfers between devices, body(): src = lax.psum(rows.astype(jnp.bfloat16), 'rcv')  33.3 us
    all_to_all x1, waiting for transfers between devices, body(): got = lax.all_to_all(pieces, 'win', 0, 0, tiled=True)  20.1 us
    dot_general x1, matrix products, body(): jnp.dot(traces.reshape(w_dev * r_dev, samples), table, preferred_element_...  11 us
    all_to_all x1, starting transfers between devices, body(): got = lax.all_to_all(pieces, 'win', 0, 0, tiled=True)  4.24 us
    mul x1, local copies, waits for them, and re-layouts, body(): return jnp.stack([real, imag], axis=2) * scale  4.1 us
    psum x1, local copies, waits for them, and re-layouts, body(): src = lax.psum(rows.astype(jnp.bfloat16), 'rcv')  3.88 us
    dot_general x1, matrix products, body(): jnp.einsum('gcwsf,gcwrf->srf', src, got, preferred_element_type=jnp.float32)  3.65 us
    dot_general x1, matrix products, body(): jnp.einsum('gcwsf,gcwrf->srf', src, turned, preferred_element_type=jnp.fl...  3.64 us
  transfers between devices with their start and end apart: 2, of which 2 were waited for; matrix products, arithmetic and copies ran while one was open for 5% of the time, Pallas kernels for 0%

commit v1 on v0

--- a/solution.py
+++ b/solution.py
@@ -37,7 +37,9 @@
     station_ids = offset + jnp.arange(r_dev, dtype=jnp.int32)
     selector = (src_station[:, None] == station_ids[None, :]).astype(jnp.bfloat16)
     rows = jnp.einsum("sr,gcwrf->gcwsf", selector, got, preferred_element_type=jnp.float32)
-    src = lax.psum(rows.astype(jnp.bfloat16), "rcv")
+    x = rows.astype(jnp.bfloat16)
+    parts = lax.all_gather(x, "rcv", axis=0, tiled=False)
+    src = parts.sum(axis=0)
     scale = 1.0 / math.sqrt(w_dev * n_win)
     turned = jnp.stack([got[:, 1], -got[:, 0]], axis=1)
     real = jnp.einsum("gcwsf,gcwrf->srf", src, got, preferred_element_type=jnp.float32)

time: 114 us -> 122 us (1.070)
  waiting for transfers between devices: 53.4 us -> 61 us
  other arithmetic: 1.54 us -> 3.51 us
    all_gather x0 -> x1, waiting for transfers between devices: none -> 41 us  [body(): parts = lax.all_gather(x, 'rcv', axis=0, tiled=False)]
    psum x1 -> x0, waiting for transfers between devices: 33.3 us -> none  [body(): src = lax.psum(rows.astype(jnp.bfloat16), 'rcv')]
    psum x1 -> x0, local copies, waits for them, and re-layouts: 3.88 us -> none  [body(): src = lax.psum(rows.astype(jnp.bfloat16), 'rcv')]
    reduce_sum x0 -> x1, local copies, waits for them, and re-layouts: none -> 2.98 us  [body(): src = parts.sum(axis=0)]
    reduce_sum x0 -> x1, other arithmetic: none -> 1.97 us  [body(): src = parts.sum(axis=0)]
where the time goes in v1:
time: 122 us
  waiting for transfers between devices  61 us (50%)
  local copies, waits for them, and re-layouts  20.3 us (17%)
  matrix products  19.5 us (16%)
  between operations  13.5 us (11%)
  starting transfers between devices  4.24 us (3%)
  other arithmetic  3.51 us (3%)
    all_gather x1, waiting for transfers between devices, body(): parts = lax.all_gather(x, 'rcv', axis=0, tiled=False)  41 us
    all_to_all x1, waiting for transfers between devices, body(): got = lax.all_to_all(pieces, 'win', 0, 0, tiled=True)  20.1 us
    dot_general x1, matrix products, body(): jnp.dot(traces.reshape(w_dev * r_dev, samples), table, preferred_element_...  11 us
    all_to_all x1, starting transfers between devices, body(): got = lax.all_to_all(pieces, 'win', 0, 0, tiled=True)  4.24 us
    mul x1, local copies, waits for them, and re-layouts, body(): return jnp.stack([real, imag], axis=2) * scale  4.1 us
    dot_general x1, matrix products, body(): jnp.einsum('gcwsf,gcwrf->srf', src, got, preferred_element_type=jnp.float32)  3.65 us
    dot_general x1, matrix products, body(): jnp.einsum('gcwsf,gcwrf->srf', src, turned, preferred_element_type=jnp.fl...  3.64 us
    reduce_sum x1, local copies, waits for them, and re-layouts, body(): src = parts.sum(axis=0)  2.98 us
  transfers between devices with their start and end apart: 2, of which 2 were waited for; matrix products, arithmetic and copies ran while one was open for 5% of the time, Pallas kernels for 0%

profile of v1, /device:TPU:0, one launch (start us, length us, event | category | flops | bytes accessed | tf_op | source)
XLA Modules:
  0.0 122.2 jit_solution(1658166313044403842)
XLA Ops:
  6.5 0.7 convert_element_type.15
  7.2 0.1 broadcast_in_dim.2
  7.3 0.1 broadcast_in_dim_reshape.3
  7.3 11.0 %multiply_reduce_fusion = (f32[768]{0:T(1024)S(1)}, f32[1024,768]{1,0:T(8,128)S(1)}) fusion(bf16[4096,1024]{1,0:T(8,128)(2,1)} %constant.19.clone, bf16[768,4096]{1,0:T(8,128)(2,1)} %bitcast.44), kind=kOutput, calls=%fused_computation.2 | convolution fusion | flops 6444022784 | bytes 17828864 | tf_op jit(solution)/shard_map/dot_general | solution.py:26
  18.4 0.3 multiply_convert_fusion
  18.7 1.3 %copy.29 = bf16[768,2,4,128]{0,3,1,2:T(8,128)(2,1)} copy(bf16[768,2,4,128]{0,3,2,1:T(8,128)(2,1)S(1)} %bitcast.42) | data formatting | bytes 3145728 | tf_op jit(solution)/shard_map/reshape | solution.py:32
  19.9 4.2 %all-to-all-start = ((bf16[4,2,768,128]{2,3,1,0:T(8,128)(2,1)}), bf16[4,2,768,128]{2,3,1,0:T(8,128)(2,1)S(1)}, u32[]{:S(2)}, u32[]{:S(2)}) async-start(bf16[4,2,768,128]{2,3,1,0:T(8,128)(2,1)} %bitcast.36), calls=%async_computation | async-start | bytes 3145728 | tf_op jit(solution)/shard_map/all_to_all | solution.py:34
  24.2 0.0 copy-start.1
  24.2 0.0 all-gather.3.cloned.1.call-start
  24.2 20.1 %all-to-all-done = bf16[4,2,768,128]{2,3,1,0:T(8,128)(2,1)S(1)} async-done(((bf16[4,2,768,128]{2,3,1,0:T(8,128)(2,1)}), bf16[4,2,768,128]{2,3,1,0:T(8,128)(2,1)S(1)}, u32[]{:S(2)}, u32[]{:S(2)}) %all-to-all-start) | async-done | bytes 1572896 | tf_op jit(solution)/shard_map/all_to_all | solution.py:34
  44.2 0.9 copy.17
  45.1 0.0 copy-done.1
  45.2 1.2 fusion
  46.4 0.0 all-gather.3.cloned.1.call-update
  46.4 3.0 %copy.18 = bf16[4,2,8,96,128]{3,2,0,1,4:T(8,128)(2,1)} copy(bf16[4,2,8,96,128]{4,3,2,1,0:T(8,128)(2,1)S(1)} %bitcast.38) | data formatting | bytes 3145728 | tf_op jit(solution)/shard_map/reshape | solution.py:35
  49.4 0.2 fusion.5
  49.5 0.1 pad_maximum_fusion
  49.7 2.9 %copy.21 = bf16[4,2,8,96,128]{3,2,0,1,4:T(8,128)(2,1)} copy(bf16[4,2,8,96,128]{4,3,2,1,0:T(8,128)(2,1)S(1)} %pad_maximum_fusion) | data formatting | bytes 3145728 | tf_op jit(solution)/shard_map/stack | solution.py:44
  52.5 41.0 %all-gather.3.cloned.1.call-done = bf16[16,2,8,32,128]{4,3,2,1,0:T(8,128)(2,1)} async-done(((bf16[4,2,8,32,128]{4,3,2,1,0:T(8,128)(2,1)}), bf16[16,2,8,32,128]{4,3,2,1,0:T(8,128)(2,1)}) %all-gather.3.cloned.1.call-update) | async-done | bytes 2097168 | tf_op jit(solution)/shard_map/all_gather | solution.py:41
  93.5 2.0 %reduce_sum.22 = bf16[4,2,8,32,128]{4,3,2,1,0:T(8,128)(2,1)S(1)} reduce(bf16[4,4,2,8,32,128]{5,4,3,2,1,0:T(8,128)(2,1)} %bitcast.43, bf16[]{:T(256)} %constant.17.clone.1), dimensions={0}, to_apply=%region_1.0 | reduce | flops 786432 | bytes 2621442 | tf_op jit(solution)/shard_map/reduce_sum | solution.py:42
  95.5 3.0 %copy.19 = bf16[4,2,8,32,128]{3,2,0,1,4:T(8,128)(2,1)S(1)} copy(bf16[4,2,8,32,128]{4,3,2,1,0:T(8,128)(2,1)S(1)} %reduce_sum.22) | data formatting | bytes 1048576 | tf_op jit(solution)/shard_map/reduce_sum | solution.py:42
  98.5 3.6 %convolution_bitcast_fusion = f32[128,96,32]{1,2,0:T(8,128)} fusion(bf16[4,2,8,96,128]{3,2,0,1,4:T(8,128)(2,1)} %copy.21, bf16[4,2,8,32,128]{3,2,0,1,4:T(8,128)(2,1)S(1)} %copy.19), kind=kOutput, calls=%fused_computation.3 | convolution fusion | flops 50331648 | bytes 3670016 | tf_op jit(solution)/shard_map/gcwsf,gcwrf->srf/dot_general | solution.py:46
  102.1 2.9 %copy.23 = f32[128,96,32]{0,1,2:T(8,128)} copy(f32[128,96,32]{1,2,0:T(8,128)} %convolution_bitcast_fusion) | data formatting | bytes 3145728 | tf_op jit(solution)/shard_map/gcwsf,gcwrf->srf/dot_general | solution.py:46
  105.0 3.6 %convolution_bitcast_fusion.1 = f32[128,96,32]{1,2,0:T(8,128)} fusion(bf16[4,2,8,96,128]{3,2,0,1,4:T(8,128)(2,1)} %copy.18, bf16[4,2,8,32,128]{3,2,0,1,4:T(8,128)(2,1)S(1)} %copy.19), kind=kOutput, calls=%fused_computation.4 | convolution fusion | flops 50331648 | bytes 3670016 | tf_op jit(solution)/shard_map/gcwsf,gcwrf->srf/dot_general | solution.py:45
  108.7 0.0 copy-start
  108.7 2.2 %copy.20 = f32[128,96,32]{0,1,2:T(8,128)S(1)} copy(f32[128,96,32]{1,2,0:T(8,128)} %convolution_bitcast_fusion.1) | data formatting | bytes 3145728 | tf_op jit(solution)/shard_map/gcwsf,gcwrf->srf/dot_general | solution.py:45
  110.9 0.0 copy-done
  110.9 0.3 maximum_multiply_fusion
  111.2 4.1 %copy.24 = f32[32,96,2,128]{3,2,1,0:T(2,128)} copy(f32[32,96,2,128]{3,1,2,0:T(8,128)S(1)} %maximum_multiply_fusion) | data formatting | bytes 6291456 | tf_op jit(solution)/shard_map/mul | solution.py:47
  (2 shorter events, 0.0 us)
Async XLA Ops:
  19.9 24.3 %all-to-all-start = ((bf16[4,2,768,128]{2,3,1,0:T(8,128)(2,1)}), bf16[4,2,768,128]{2,3,1,0:T(8,128)(2,1)S(1)}, u32[]{:S(2)}, u32[]{:S(2)}) async-start(bf16[4,2,768,128]{2,3,1,0:T(8,128)(2,1)} %bitcast.36), calls=%async_computation | async-start | bytes 3145728 | tf_op jit(solution)/shard_map/all_to_all | solution.py:34
  24.2 21.0 %copy-start.1 = (s32[32]{0:T(128)S(1)}, s32[32]{0:T(128)}, u32[]{:S(2)}) copy-start(s32[32]{0:T(128)} %param.6) | copy-start | bytes 388
  24.2 69.3 %all-gather.3.cloned.1.call-start = ((), (), s32[]{:S(2)}) async-start(), calls=%async_computation.1 | async-start | bytes 2621440 | tf_op jit(solution)/shard_map/all_gather | solution.py:41
  108.7 2.2 %copy-start = (f32[128,96,32]{0,1,2:T(8,128)S(1)}, f32[128,96,32]{0,1,2:T(8,128)}, u32[]{:S(2)}) copy-start(f32[128,96,32]{0,1,2:T(8,128)} %copy.23) | copy-start | bytes 4718596
Sparse Core Ops, SparseCore 0:
  46.5 46.9 all-gather.2
